TPU v7x, 256 devices: a whole 4x4x8 slice. The times are simulated.
256 devices in a mesh: group: 32 (over z, x), member: 4 (over y), pair: 2 (over core).
Axes of the slice: x: 4, y: 4, z: 8, core: 2. Of those that a mesh axis runs over, the one named last changes fastest.
Arguments:
- tokens: bfloat16 [32768, 768], P(('group', 'member', 'pair')), may hold values from -6 to 6
- out_grad: bfloat16 [32768, 768], P(('group', 'member', 'pair')), may hold values from -6 to 6
- router_gate: float32 [32768], P(('group', 'member', 'pair')), may hold values from 0.2 to 1
- expand_weight: bfloat16 [128, 768, 3072], P(('group', 'member'), None, 'pair'), may hold values from -0.21875 to 0.21875
- shrink_weight: bfloat16 [128, 3072, 768], P(('group', 'member'), 'pair'), may hold values from -0.109375 to 0.109375
- expert_ids: int32 [32768], P(('group', 'member', 'pair')), may hold values from 0 to 127, as said below
- slot_ids: int32 [32768], P(('group', 'member', 'pair')), may hold values from 0 to 1, as said below
- capacity: int32 [128], replicated, may hold values from 1 to 2, as said below
Outputs:
- token_grad: bfloat16 [32768, 768], P(('group', 'member', 'pair'))
- expand_grad: bfloat16 [128, 768, 3072], P(('group', 'member'), None, 'pair')
- shrink_grad: bfloat16 [128, 3072, 768], P(('group', 'member'), 'pair')
Inputs may be any that keep to these rules, and one draw needn't show every extreme that they name: `expert_ids`: in each aligned block of 128 tokens (the tokens of one device) no expert is named by more than 2 tokens, and one expert, the same for all blocks, is named by exactly 2 tokens in every block. `slot_ids`: A token's slot is the number of earlier tokens of its aligned block of 128 that name the same expert. The expert that is named 2 times in every block has capacity 2.
All inputs are finite; a program needn't handle non-finite values.
Results may differ from a plain program's by a relative error of at most 0.0058.
Values may be sent and summed in bfloat16 or wider, within the bound.
A program may use at most 64 MiB of HBM per device.

v0:
```python
import jax
import jax.numpy as jnp
from jax import lax
from jax.sharding import PartitionSpec as P


def activation(value):
    return jax.nn.gelu(value, approximate=True)


def expert_pass(token_rows, grad_rows, expand, shrink):
    f32 = jnp.float32
    preact = jnp.einsum("rd,df->rf", token_rows, expand, preferred_element_type=f32)
    hidden, pullback = jax.vjp(activation, preact)
    hidden_low = hidden.astype(jnp.bfloat16)
    post_grad = jnp.einsum("rd,fd->rf", grad_rows, shrink, preferred_element_type=f32)
    pre_grad = pullback(post_grad)[0].astype(jnp.bfloat16)
    partial_value = jnp.einsum("rf,df->rd", pre_grad, expand, preferred_element_type=f32)
    expand_part = jnp.einsum("rd,rf->df", token_rows, pre_grad, preferred_element_type=f32)
    shrink_part = jnp.einsum("rf,rd->fd", hidden_low, grad_rows, preferred_element_type=f32)
    return (expand_part.astype(jnp.bfloat16), shrink_part.astype(jnp.bfloat16), partial_value)


def per_device(
    tokens, out_grad, router_gate, expand_weight, shrink_weight, expert_ids, slot_ids, capacity
):
    tok_dev, width = tokens.shape
    experts = capacity.shape[0]
    slots = max(2, 2 * tok_dev // experts)
    f32, bf16 = (jnp.float32, jnp.bfloat16)
    table = jnp.arange(experts, dtype=jnp.int32)
    limits = jnp.sum(jnp.where(expert_ids[:, None] == table[None, :], capacity[None, :], 0), axis=1)
    keep = slot_ids < limits
    target = jnp.where(keep, expert_ids * slots + slot_ids, experts * slots)
    place = (jnp.arange(experts * slots, dtype=jnp.int32)[:, None] == target[None, :]).astype(bf16)
    scaled = (router_gate[:, None] * out_grad.astype(f32)).astype(bf16)
    token_send = jnp.dot(place, tokens, preferred_element_type=f32).astype(bf16)
    grad_send = jnp.dot(place, scaled, preferred_element_type=f32).astype(bf16)
    token_send = token_send.reshape(experts, slots, width)
    grad_send = grad_send.reshape(experts, slots, width)
    axes = ("group", "member")
    token_rows = lax.all_to_all(token_send, axes, split_axis=0, concat_axis=0, tiled=True)
    grad_rows = lax.all_to_all(grad_send, axes, split_axis=0, concat_axis=0, tiled=True)
    token_rows = lax.all_gather(token_rows.reshape(-1, width), "pair", axis=0, tiled=True)
    grad_rows = lax.all_gather(grad_rows.reshape(-1, width), "pair", axis=0, tiled=True)
    expand_grad, shrink_grad, partial_value = expert_pass(
        token_rows, grad_rows, expand_weight[0], shrink_weight[0]
    )
    rows = experts * slots
    me = lax.axis_index("pair")
    halves = partial_value.reshape(2, rows, width)
    other = lax.ppermute(
        lax.dynamic_index_in_dim(halves, 1 - me, 0, keepdims=False), "pair", ((0, 1), (1, 0))
    )
    summed = lax.dynamic_index_in_dim(halves, me, 0, keepdims=False) + other
    back = summed.astype(bf16).reshape(experts, slots, width)
    back = lax.all_to_all(back, axes, split_axis=0, concat_axis=0, tiled=True)
    token_grad = lax.dot_general(
        place, back.reshape(rows, width), (((0,), (0,)), ((), ())), preferred_element_type=f32
    ).astype(bf16)
    return (token_grad, expand_grad[None], shrink_grad[None])


def solution(mesh):
    placed = (
        P(("group", "member", "pair"), None),
        P(("group", "member", "pair"), None),
        P(("group", "member", "pair")),
        P(("group", "member"), None, "pair"),
        P(("group", "member"), "pair", None),
        P(("group", "member", "pair")),
        P(("group", "member", "pair")),
        P(),
    )
    return jax.shard_map(
        per_device,
        mesh=mesh,
        in_specs=placed,
        out_specs=(
            P(("group", "member", "pair"), None),
            P(("group", "member"), None, "pair"),
            P(("group", "member"), "pair", None),
        ),
        check_vma=False,
    )
```

profile of v0, /device:TPU:1, one launch (start us, length us, event | category | flops | bytes accessed | tf_op | source)
XLA Modules:
  0.0 102.9 jit_solution(17785780471842416386)
XLA Ops:
  0.6 1.0 select_reduce_fusion
  2.3 1.2 %convolution_convert_fusion.2 = bf16[256,768]{1,0:T(8,128)(2,1)S(1)} fusion(bf16[128,768]{1,0:T(8,128)(2,1)} %param.8, s32[128]{0:T(128)S(1)} %compare_select_fusion), kind=kOutput, calls=%fused_computation.24 | convolution fusion | flops 50561024 | bytes 590336 | tf_op jit(solution)/shard_map/dot_general | solution.py:37
  3.5 0.9 reshape.32
  4.4 16.3 %all-to-all-start.1 = ((bf16[128,2,768]{2,1,0:T(2,128)(2,1)}), bf16[128,2,768]{2,1,0:T(2,128)(2,1)S(1)}, u32[]{:S(2)}, u32[]{:S(2)}) async-start(bf16[128,2,768]{2,1,0:T(2,128)(2,1)} %reshape.32), calls=%async_computation.1 | async-start | bytes 786432 | tf_op jit(solution)/shard_map/all_to_all | solution.py:42
  20.7 1.3 %convolution_convert_fusion.3 = bf16[256,768]{1,0:T(8,128)(2,1)S(1)} fusion(bf16[128,768]{1,0:T(8,128)(2,1)} %param.9, f32[128]{0:T(128)} %param.10, s32[128]{0:T(128)S(1)} %compare_select_fusion), kind=kOutput, calls=%fused_computation.25 | convolution fusion | flops 50855936 | bytes 590848 | tf_op jit(solution)/shard_map/dot_general | solution.py:38
  22.0 0.9 reshape.30
  22.9 13.8 %all-to-all-done.1 = bf16[128,2,768]{2,1,0:T(2,128)(2,1)S(1)} async-done(((bf16[128,2,768]{2,1,0:T(2,128)(2,1)}), bf16[128,2,768]{2,1,0:T(2,128)(2,1)S(1)}, u32[]{:S(2)}, u32[]{:S(2)}) %all-to-all-start.1) | async-done | bytes 393248 | tf_op jit(solution)/shard_map/all_to_all | solution.py:42
  36.7 6.8 %all-to-all-start = ((bf16[128,2,768]{2,1,0:T(2,128)(2,1)}), bf16[128,2,768]{2,1,0:T(2,128)(2,1)S(1)}, u32[]{:S(2)}, u32[]{:S(2)}) async-start(bf16[128,2,768]{2,1,0:T(2,128)(2,1)} %reshape.30), calls=%async_computation | async-start | bytes 786432 | tf_op jit(solution)/shard_map/all_to_all | solution.py:43
  43.7 4.4 %all_gather.7 = bf16[512,768]{1,0:T(8,128)(2,1)} all-gather(bf16[256,768]{1,0:T(8,128)(2,1)S(1)} %reshape.33), channel_id=1, replica_groups=mesh['group'=32,'member'=4,'pair'=2] {'pair'}, dimensions={0}, use_global_device_ids=true | all-gather | bytes 1179648 | tf_op jit(solution)/shard_map/all_gather | solution.py:44
  48.1 9.8 %all-to-all-done = bf16[128,2,768]{2,1,0:T(2,128)(2,1)S(1)} async-done(((bf16[128,2,768]{2,1,0:T(2,128)(2,1)}), bf16[128,2,768]{2,1,0:T(2,128)(2,1)S(1)}, u32[]{:S(2)}, u32[]{:S(2)}) %all-to-all-start) | async-done | bytes 393248 | tf_op jit(solution)/shard_map/all_to_all | solution.py:43
  58.1 6.4 %all_gather.6 = bf16[512,768]{1,0:T(8,128)(2,1)S(1)} all-gather(bf16[256,768]{1,0:T(8,128)(2,1)S(1)} %reshape.31), channel_id=1, replica_groups=mesh['group'=32,'member'=4,'pair'=2] {'pair'}, dimensions={0}, use_global_device_ids=true | all-gather | bytes 1179648 | tf_op jit(solution)/shard_map/all_gather | solution.py:45
  64.5 2.9 %fusion.11 = f32[512,1536]{1,0:T(8,128)S(1)} fusion(bf16[512,768]{1,0:T(8,128)(2,1)} %all_gather.7, bf16[1,768,1536]{2,1,0:T(8,128)(2,1)S(1)} %copy-done), kind=kOutput, calls=%fused_computation.16 | convolution fusion | flops 1207959552 | bytes 6291456 | tf_op jit(solution)/shard_map/rd,df->rf/dot_general | solution.py:13
  67.4 3.1 %fusion.6 = bf16[512,1536]{1,0:T(8,128)(2,1)S(1)} fusion(f32[512,1536]{1,0:T(8,128)S(1)} %fusion.11, bf16[512,768]{1,0:T(8,128)(2,1)S(1)} %all_gather.6, bf16[1,1536,768]{2,1,0:T(8,128)(2,1)S(1)} %copy-done.5), kind=kOutput, calls=%fused_computation.10 | convolution fusion | flops 1223688192 | bytes 7864320 | tf_op jit(solution)/shard_map/rd,fd->rf/dot_general | solution.py:16
  70.5 1.4 %fusion.9 = f32[2,256,768]{2,1,0:T(8,128)S(1)} fusion(bf16[2,256,1536]{2,1,0:T(8,128)(2,1)S(1)} %bitcast.30, bf16[1,768,1536]{2,1,0:T(8,128)(2,1)S(1)} %copy-done), kind=kOutput, calls=%fused_computation.14 | convolution fusion | flops 1207959552 | bytes 5505024 | tf_op jit(solution)/shard_map/rf,df->rd/dot_general | solution.py:18
  72.0 1.1 %copy-done.1 = f32[2,256,768]{2,1,0:T(8,128)} copy-done((f32[2,256,768]{2,1,0:T(8,128)}, f32[2,256,768]{2,1,0:T(8,128)S(1)}, u32[]{:S(2)}) %copy-start.1) | copy-done | bytes 1572888
  73.1 0.9 dynamic-slice_bitcast_fusion
  74.4 2.3 %collective-permute-done = f32[256,768]{1,0:T(8,128)} collective-permute-done((f32[256,768]{1,0:T(8,128)}, f32[256,768]{1,0:T(8,128)}, u32[]{:S(2)}, u32[]{:S(2)}) %collective-permute-start) | collective-permute-done | bytes 786464 | tf_op jit(solution)/shard_map/ppermute | solution.py:52
  76.7 1.4 %fusion.21 = bf16[256,768]{1,0:T(8,128)(2,1)S(1)} fusion(f32[256,768]{1,0:T(8,128)} %collective-permute-done, f32[2,256,768]{2,1,0:T(8,128)} %copy-done.1, s32[]{:T(128)S(6)} %select_n.17), kind=kLoop, calls=%fused_computation.28 | loop fusion | flops 393216 | bytes 1966084 | tf_op jit(solution)/shard_map/convert_element_type | solution.py:56
  78.1 0.9 reshape.34
  79.0 6.3 %all-to-all-start.2 = ((bf16[128,2,768]{2,1,0:T(2,128)(2,1)}), bf16[128,2,768]{2,1,0:T(2,128)(2,1)S(1)}, u32[]{:S(2)}, u32[]{:S(2)}) async-start(bf16[128,2,768]{2,1,0:T(2,128)(2,1)} %reshape.34), calls=%async_computation.2 | async-start | bytes 786432 | tf_op jit(solution)/shard_map/all_to_all | solution.py:57
  85.4 4.4 %fusion.7 = bf16[1,768,1536]{2,1,0:T(8,128)(2,1)} fusion(bf16[512,768]{1,0:T(8,128)(2,1)S(1)} %copy-done.2, bf16[512,1536]{1,0:T(8,128)(2,1)} %copy-done.6), kind=kOutput, calls=%fused_computation.12 | convolution fusion | flops 1209139200 | bytes 4718592 | tf_op jit(solution)/shard_map/rd,rf->df/dot_general | solution.py:19
  89.8 3.2 %fusion.8 = bf16[1,1536,768]{2,1,0:T(8,128)(2,1)} fusion(bf16[512,768]{1,0:T(8,128)(2,1)S(1)} %copy-done.4, f32[512,1536]{1,0:T(8,128)S(1)} %copy-done.8), kind=kOutput, calls=%fused_computation.13 | convolution fusion | flops 1216217088 | bytes 6291456 | tf_op jit(solution)/shard_map/rf,rd->fd/dot_general | solution.py:20
  93.0 8.8 %all-to-all-done.2 = bf16[128,2,768]{2,1,0:T(2,128)(2,1)S(1)} async-done(((bf16[128,2,768]{2,1,0:T(2,128)(2,1)}), bf16[128,2,768]{2,1,0:T(2,128)(2,1)S(1)}, u32[]{:S(2)}, u32[]{:S(2)}) %all-to-all-start.2) | async-done | bytes 393248 | tf_op jit(solution)/shard_map/all_to_all | solution.py:57
  101.9 0.9 convolution_convert_fusion.4
  (22 shorter events, 1.5 us)
Async XLA Ops:
  0.6 63.9 %copy-start = (bf16[1,768,1536]{2,1,0:T(8,128)(2,1)S(1)}, bf16[1,768,1536]{2,1,0:T(8,128)(2,1)}, u32[]{:S(2)}) copy-start(bf16[1,768,1536]{2,1,0:T(8,128)(2,1)} %param.11) | copy-start | bytes 7077892
  4.4 32.3 %all-to-all-start.1 = ((bf16[128,2,768]{2,1,0:T(2,128)(2,1)}), bf16[128,2,768]{2,1,0:T(2,128)(2,1)S(1)}, u32[]{:S(2)}, u32[]{:S(2)}) async-start(bf16[128,2,768]{2,1,0:T(2,128)(2,1)} %reshape.32), calls=%async_computation.1 | async-start | bytes 786432 | tf_op jit(solution)/shard_map/all_to_all | solution.py:42
  36.7 21.3 %all-to-all-start = ((bf16[128,2,768]{2,1,0:T(2,128)(2,1)}), bf16[128,2,768]{2,1,0:T(2,128)(2,1)S(1)}, u32[]{:S(2)}, u32[]{:S(2)}) async-start(bf16[128,2,768]{2,1,0:T(2,128)(2,1)} %reshape.30), calls=%async_computation | async-start | bytes 786432 | tf_op jit(solution)/shard_map/all_to_all | solution.py:43
  64.5 2.9 %copy-start.3 = (bf16[512,768]{1,0:T(8,128)(2,1)}, bf16[512,768]{1,0:T(8,128)(2,1)S(1)}, u32[]{:S(2)}) copy-start(bf16[512,768]{1,0:T(8,128)(2,1)S(1)} %all_gather.6) | copy-start | bytes 2359300
  64.5 2.9 %copy-start.5 = (bf16[1,1536,768]{2,1,0:T(8,128)(2,1)S(1)}, bf16[1,1536,768]{2,1,0:T(8,128)(2,1)}, u32[]{:S(2)}) copy-start(bf16[1,1536,768]{2,1,0:T(8,128)(2,1)} %param.12) | copy-start | bytes 7077892
  67.4 3.1 %copy-start.7 = (f32[512,1536]{1,0:T(8,128)}, f32[512,1536]{1,0:T(8,128)S(1)}, u32[]{:S(2)}) copy-start(f32[512,1536]{1,0:T(8,128)S(1)} %fusion.11) | copy-start | bytes 9437188
  70.5 1.4 %copy-start.6 = (bf16[512,1536]{1,0:T(8,128)(2,1)}, bf16[512,1536]{1,0:T(8,128)(2,1)S(1)}, u32[]{:S(2)}) copy-start(bf16[512,1536]{1,0:T(8,128)(2,1)S(1)} %fusion.6) | copy-start | bytes 4718596
  72.0 1.1 %copy-start.1 = (f32[2,256,768]{2,1,0:T(8,128)}, f32[2,256,768]{2,1,0:T(8,128)S(1)}, u32[]{:S(2)}) copy-start(f32[2,256,768]{2,1,0:T(8,128)S(1)} %fusion.9) | copy-start | bytes 4718596
  73.1 12.3 %copy-start.2 = (bf16[512,768]{1,0:T(8,128)(2,1)S(1)}, bf16[512,768]{1,0:T(8,128)(2,1)}, u32[]{:S(2)}) copy-start(bf16[512,768]{1,0:T(8,128)(2,1)} %all_gather.7) | copy-start | bytes 2359300
  74.0 2.6 %collective-permute-start = (f32[256,768]{1,0:T(8,128)}, f32[256,768]{1,0:T(8,128)}, u32[]{:S(2)}, u32[]{:S(2)}) collective-permute-start(f32[256,768]{1,0:T(8,128)} %dynamic-slice_bitcast_fusion), channel_id=1, source_target_pairs={{0,1},{1,0},{2,3},{3,2},{4,5},{5,4},{6,7},{7,6},{8,9},{9,8},{10,11... | collective-permute-start | bytes 2359304 | tf_op jit(solution)/shard_map/ppermute | solution.py:52
  79.0 22.8 %all-to-all-start.2 = ((bf16[128,2,768]{2,1,0:T(2,128)(2,1)}), bf16[128,2,768]{2,1,0:T(2,128)(2,1)S(1)}, u32[]{:S(2)}, u32[]{:S(2)}) async-start(bf16[128,2,768]{2,1,0:T(2,128)(2,1)} %reshape.34), calls=%async_computation.2 | async-start | bytes 786432 | tf_op jit(solution)/shard_map/all_to_all | solution.py:57
  85.4 4.4 %copy-start.4 = (bf16[512,768]{1,0:T(8,128)(2,1)S(1)}, bf16[512,768]{1,0:T(8,128)(2,1)}, u32[]{:S(2)}) copy-start(bf16[512,768]{1,0:T(8,128)(2,1)} %copy-done.3) | copy-start | bytes 2359300
  85.4 4.4 %copy-start.8 = (f32[512,1536]{1,0:T(8,128)S(1)}, f32[512,1536]{1,0:T(8,128)}, u32[]{:S(2)}) copy-start(f32[512,1536]{1,0:T(8,128)} %copy-done.7) | copy-start | bytes 9437188
where the time goes:
time: 103 us
  waiting for transfers between devices  34.7 us (34%)
  starting transfers between devices  29.9 us (29%)
  matrix products  18.2 us (18%)
  blocking collectives  10.9 us (11%)
  local copies, waits for them, and re-layouts  5.25 us (5%)
  other arithmetic  3.12 us (3%)
    all_to_all x1, starting transfers between devices, per_device(): lax.all_to_all(token_send, axes, split_axis=0, concat_axis=0, tiled=True)  16.3 us
    all_to_all x1, waiting for transfers between devices, per_device(): lax.all_to_all(token_send, axes, split_axis=0, concat_axis=0, tiled=True)  13.8 us
    all_to_all x1, waiting for transfers between devices, per_device(): lax.all_to_all(grad_send, axes, split_axis=0, concat_axis=0, tiled=True)  9.84 us
    all_to_all x1, waiting for transfers between devices, per_device(): back = lax.all_to_all(back, axes, split_axis=0, concat_axis=0, tiled=True)  8.84 us
    all_to_all x1, starting transfers between devices, per_device(): lax.all_to_all(grad_send, axes, split_axis=0, concat_axis=0, tiled=True)  6.83 us
    all_gather x1, blocking collectives, per_device(): lax.all_gather(grad_rows.reshape(-1, width), 'pair', axis=0, tiled=True)  6.43 us
    all_to_all x1, starting transfers between devices, per_device(): back = lax.all_to_all(back, axes, split_axis=0, concat_axis=0, tiled=True)  6.35 us
    all_gather x1, blocking collectives, per_device(): lax.all_gather(token_rows.reshape(-1, width), 'pair', axis=0, tiled=True)  4.44 us
  transfers between devices with their start and end apart: 4, of which 4 were waited for; matrix products, arithmetic and copies ran while one was open for 10% of the time, Pallas kernels for 0%

commit v1 on v0

--- a/solution.py
+++ b/solution.py
@@ -2,6 +2,13 @@
 import jax.numpy as jnp
 from jax import lax
 from jax.sharding import PartitionSpec as P
+
+
+def all_by_exchange(x, mesh_axis, along):
+    size = lax.axis_size(mesh_axis)
+    blocks = jnp.stack([x for _ in range(size)])
+    blocks = lax.all_to_all(blocks, mesh_axis, split_axis=0, concat_axis=0)
+    return jnp.concatenate(blocks, axis=along)
 
 
 def activation(value):
@@ -42,7 +49,7 @@
     token_rows = lax.all_to_all(token_send, axes, split_axis=0, concat_axis=0, tiled=True)
     grad_rows = lax.all_to_all(grad_send, axes, split_axis=0, concat_axis=0, tiled=True)
     token_rows = lax.all_gather(token_rows.reshape(-1, width), "pair", axis=0, tiled=True)
-    grad_rows = lax.all_gather(grad_rows.reshape(-1, width), "pair", axis=0, tiled=True)
+    grad_rows = all_by_exchange(grad_rows.reshape(-1, width), "pair", 0)
     expand_grad, shrink_grad, partial_value = expert_pass(
         token_rows, grad_rows, expand_weight[0], shrink_weight[0]
     )

time: 103 us -> 110 us (1.068)
  starting transfers between devices: 29.9 us -> 37.5 us
  blocking collectives: 10.9 us -> 4.44 us
  matrix products: 18.2 us -> 21.8 us
    all_to_all x0 -> x1, starting transfers between devices: none -> 7.96 us  [all_by_exchange(): blocks = lax.all_to_all(blocks, mesh_axis, split_axis=0, concat_axis=0)]
    all_gather x1 -> x0, blocking collectives: 6.43 us -> none  [per_device(): lax.all_gather(grad_rows.reshape(-1, width), 'pair', axis=0, tiled=True)]
    dot_general x1, matrix products: 3.07 us -> 5.32 us  [expert_pass(): jnp.einsum('rd,fd->rf', grad_rows, shrink, preferred_element_type=f32)]
    dot_general x1, matrix products: 2.85 us -> 4.15 us  [expert_pass(): jnp.einsum('rd,df->rf', token_rows, expand, preferred_element_type=f32)]
  transfers between devices with their start and end apart: 4 -> 5, of which waited for: 4 -> 4; matrix products, arithmetic and copies ran while one was open for 10% -> 13% of each run, Pallas kernels for 0% -> 0%
where the time goes in v1:
time: 110 us; the launch traced here: 109 us
  starting transfers between devices  37.5 us (34%)
  waiting for transfers between devices  35.3 us (32%)
  matrix products  21.8 us (20%)
  local copies, waits for them, and re-layouts  5.24 us (5%)
  blocking collectives  4.44 us (4%)
  other arithmetic  4.06 us (4%)
    all_to_all x1, starting transfers between devices, per_device(): lax.all_to_all(token_send, axes, split_axis=0, concat_axis=0, tiled=True)  16.3 us
    all_to_all x1, waiting for transfers between devices, per_device(): lax.all_to_all(token_send, axes, split_axis=0, concat_axis=0, tiled=True)  13.8 us
    all_to_all x1, waiting for transfers between devices, per_device(): lax.all_to_all(grad_send, axes, split_axis=0, concat_axis=0, tiled=True)  9.84 us
    all_to_all x1, waiting for transfers between devices, per_device(): back = lax.all_to_all(back, axes, split_axis=0, concat_axis=0, tiled=True)  9.06 us
    all_to_all x1, starting transfers between devices, all_by_exchange(): blocks = lax.all_to_all(blocks, mesh_axis, split_axis=0, concat_axis=0)  7.96 us
    all_to_all x1, starting transfers between devices, per_device(): lax.all_to_all(grad_send, axes, split_axis=0, concat_axis=0, tiled=True)  6.83 us
    all_to_all x1, starting transfers between devices, per_device(): back = lax.all_to_all(back, axes, split_axis=0, concat_axis=0, tiled=True)  6.35 us
    dot_general x1, matrix products, expert_pass(): jnp.einsum('rd,fd->rf', grad_rows, shrink, preferred_element_type=f32)  5.32 us
  transfers between devices with their start and end apart: 5, of which 4 were waited for; matrix products, arithmetic and copies ran while one was open for 13% of the time, Pallas kernels for 0%

profile of v1, /device:TPU:1, one launch (start us, length us, event | category | flops | bytes accessed | tf_op | source)
XLA Modules:
  0.0 109.1 jit_solution(6240009053933556374)
XLA Ops:
  0.6 1.0 select_reduce_fusion
  2.3 1.2 %convolution_convert_fusion.2 = bf16[256,768]{1,0:T(8,128)(2,1)S(1)} fusion(bf16[128,768]{1,0:T(8,128)(2,1)} %param.8, s32[128]{0:T(128)S(1)} %compare_select_fusion), kind=kOutput, calls=%fused_computation.24 | convolution fusion | flops 50561024 | bytes 590336 | tf_op jit(solution)/shard_map/dot_general | solution.py:44
  3.5 0.9 reshape.32
  4.4 16.3 %all-to-all-start.2 = ((bf16[128,2,768]{2,1,0:T(2,128)(2,1)}), bf16[128,2,768]{2,1,0:T(2,128)(2,1)S(1)}, u32[]{:S(2)}, u32[]{:S(2)}) async-start(bf16[128,2,768]{2,1,0:T(2,128)(2,1)} %reshape.32), calls=%async_computation.2 | async-start | bytes 786432 | tf_op jit(solution)/shard_map/all_to_all | solution.py:49
  20.7 1.3 %convolution_convert_fusion.3 = bf16[256,768]{1,0:T(8,128)(2,1)S(1)} fusion(bf16[128,768]{1,0:T(8,128)(2,1)} %param.9, f32[128]{0:T(128)} %param.10, s32[128]{0:T(128)S(1)} %compare_select_fusion), kind=kOutput, calls=%fused_computation.25 | convolution fusion | flops 50855936 | bytes 590848 | tf_op jit(solution)/shard_map/dot_general | solution.py:45
  22.9 13.8 %all-to-all-done.2 = bf16[128,2,768]{2,1,0:T(2,128)(2,1)S(1)} async-done(((bf16[128,2,768]{2,1,0:T(2,128)(2,1)}), bf16[128,2,768]{2,1,0:T(2,128)(2,1)S(1)}, u32[]{:S(2)}, u32[]{:S(2)}) %all-to-all-start.2) | async-done | bytes 393248 | tf_op jit(solution)/shard_map/all_to_all | solution.py:49
  36.7 6.8 %all-to-all-start = ((bf16[128,2,768]{2,1,0:T(2,128)(2,1)}), bf16[128,2,768]{2,1,0:T(2,128)(2,1)S(1)}, u32[]{:S(2)}, u32[]{:S(2)}) async-start(bf16[128,2,768]{2,1,0:T(2,128)(2,1)} %reshape.30), calls=%async_computation | async-start | bytes 786432 | tf_op jit(solution)/shard_map/all_to_all | solution.py:50
  43.7 4.4 %all_gather.3 = bf16[512,768]{1,0:T(8,128)(2,1)} all-gather(bf16[256,768]{1,0:T(8,128)(2,1)S(1)} %reshape.33), channel_id=1, replica_groups=mesh['group'=32,'member'=4,'pair'=2] {'pair'}, dimensions={0}, use_global_device_ids=true | all-gather | bytes 1179648 | tf_op jit(solution)/shard_map/all_gather | solution.py:51
  48.1 9.8 %all-to-all-done = bf16[128,2,768]{2,1,0:T(2,128)(2,1)S(1)} async-done(((bf16[128,2,768]{2,1,0:T(2,128)(2,1)}), bf16[128,2,768]{2,1,0:T(2,128)(2,1)S(1)}, u32[]{:S(2)}, u32[]{:S(2)}) %all-to-all-start) | async-done | bytes 393248 | tf_op jit(solution)/shard_map/all_to_all | solution.py:50
  58.1 0.9 pad_maximum_fusion
  59.0 8.0 %all-to-all-start.1 = ((bf16[2,256,768]{2,1,0:T(8,128)(2,1)}), bf16[2,256,768]{2,1,0:T(8,128)(2,1)S(1)}, u32[]{:S(2)}, u32[]{:S(2)}) async-start(bf16[2,256,768]{2,1,0:T(8,128)(2,1)} %pad_maximum_fusion), calls=%async_computation.1 | async-start | bytes 1572864 | tf_op jit(solution)/shard_map/all_to_all | solution.py:10
  67.0 4.2 %fusion.11 = f32[512,1536]{1,0:T(8,128)} fusion(bf16[512,768]{1,0:T(8,128)(2,1)} %all_gather.3, bf16[1,768,1536]{2,1,0:T(8,128)(2,1)S(1)} %copy-done), kind=kOutput, calls=%fused_computation.16 | convolution fusion | flops 1207959552 | bytes 6291456 | tf_op jit(solution)/shard_map/rd,df->rf/dot_general | solution.py:20
  71.2 5.3 %fusion.6 = bf16[512,1536]{1,0:T(8,128)(2,1)S(1)} fusion(f32[512,1536]{1,0:T(8,128)} %fusion.11, bf16[512,768]{1,0:T(8,128)(2,1)S(1)} %bitcast.31, bf16[1,1536,768]{2,1,0:T(8,128)(2,1)} %param.12), kind=kOutput, calls=%fused_computation.10 | convolution fusion | flops 1223688192 | bytes 7864320 | tf_op jit(solution)/shard_map/rd,fd->rf/dot_general | solution.py:23
  76.5 1.4 %fusion.9 = f32[2,256,768]{2,1,0:T(8,128)S(1)} fusion(bf16[2,256,1536]{2,1,0:T(8,128)(2,1)S(1)} %bitcast.33, bf16[1,768,1536]{2,1,0:T(8,128)(2,1)S(1)} %copy-done), kind=kOutput, calls=%fused_computation.14 | convolution fusion | flops 1207959552 | bytes 5505024 | tf_op jit(solution)/shard_map/rf,df->rd/dot_general | solution.py:25
  78.0 1.1 %copy-done.1 = f32[2,256,768]{2,1,0:T(8,128)} copy-done((f32[2,256,768]{2,1,0:T(8,128)}, f32[2,256,768]{2,1,0:T(8,128)S(1)}, u32[]{:S(2)}) %copy-start.1) | copy-done | bytes 1572888
  79.1 0.9 dynamic-slice_bitcast_fusion
  80.1 2.6 %collective-permute-done = f32[256,768]{1,0:T(8,128)} collective-permute-done((f32[256,768]{1,0:T(8,128)}, f32[256,768]{1,0:T(8,128)}, u32[]{:S(2)}, u32[]{:S(2)}) %collective-permute-start) | collective-permute-done | bytes 786464 | tf_op jit(solution)/shard_map/ppermute | solution.py:59
  82.7 1.4 %fusion.21 = bf16[256,768]{1,0:T(8,128)(2,1)S(1)} fusion(f32[256,768]{1,0:T(8,128)} %collective-permute-done, f32[2,256,768]{2,1,0:T(8,128)} %copy-done.1, s32[]{:T(128)S(6)} %select_n.17), kind=kLoop, calls=%fused_computation.29 | loop fusion | flops 393216 | bytes 1966084 | tf_op jit(solution)/shard_map/convert_element_type | solution.py:63
  84.1 0.9 reshape.34
  85.0 6.3 %all-to-all-start.3 = ((bf16[128,2,768]{2,1,0:T(2,128)(2,1)}), bf16[128,2,768]{2,1,0:T(2,128)(2,1)S(1)}, u32[]{:S(2)}, u32[]{:S(2)}) async-start(bf16[128,2,768]{2,1,0:T(2,128)(2,1)} %reshape.34), calls=%async_computation.3 | async-start | bytes 786432 | tf_op jit(solution)/shard_map/all_to_all | solution.py:64
  91.4 4.4 %fusion.7 = bf16[1,768,1536]{2,1,0:T(8,128)(2,1)} fusion(bf16[512,768]{1,0:T(8,128)(2,1)S(1)} %copy-done.2, bf16[512,1536]{1,0:T(8,128)(2,1)} %copy-done.5), kind=kOutput, calls=%fused_computation.12 | convolution fusion | flops 1209139200 | bytes 4718592 | tf_op jit(solution)/shard_map/rd,rf->df/dot_general | solution.py:26
  95.8 3.2 %fusion.8 = bf16[1,1536,768]{2,1,0:T(8,128)(2,1)} fusion(bf16[512,768]{1,0:T(8,128)(2,1)S(1)} %bitcast.32, f32[512,1536]{1,0:T(8,128)S(1)} %copy-done.6), kind=kOutput, calls=%fused_computation.13 | convolution fusion | flops 1216217088 | bytes 6291456 | tf_op jit(solution)/shard_map/rf,rd->fd/dot_general | solution.py:27
  98.9 9.1 %all-to-all-done.3 = bf16[128,2,768]{2,1,0:T(2,128)(2,1)S(1)} async-done(((bf16[128,2,768]{2,1,0:T(2,128)(2,1)}), bf16[128,2,768]{2,1,0:T(2,128)(2,1)S(1)}, u32[]{:S(2)}, u32[]{:S(2)}) %all-to-all-start.3) | async-done | bytes 393248 | tf_op jit(solution)/shard_map/all_to_all | solution.py:64
  108.1 0.9 convolution_convert_fusion.4
  (20 shorter events, 2.1 us)
Async XLA Ops:
  0.6 66.4 %copy-start = (bf16[1,768,1536]{2,1,0:T(8,128)(2,1)S(1)}, bf16[1,768,1536]{2,1,0:T(8,128)(2,1)}, u32[]{:S(2)}) copy-start(bf16[1,768,1536]{2,1,0:T(8,128)(2,1)} %param.11) | copy-start | bytes 7077892
  4.4 32.3 %all-to-all-start.2 = ((bf16[128,2,768]{2,1,0:T(2,128)(2,1)}), bf16[128,2,768]{2,1,0:T(2,128)(2,1)S(1)}, u32[]{:S(2)}, u32[]{:S(2)}) async-start(bf16[128,2,768]{2,1,0:T(2,128)(2,1)} %reshape.32), calls=%async_computation.2 | async-start | bytes 786432 | tf_op jit(solution)/shard_map/all_to_all | solution.py:49
  36.7 21.3 %all-to-all-start = ((bf16[128,2,768]{2,1,0:T(2,128)(2,1)}), bf16[128,2,768]{2,1,0:T(2,128)(2,1)S(1)}, u32[]{:S(2)}, u32[]{:S(2)}) async-start(bf16[128,2,768]{2,1,0:T(2,128)(2,1)} %reshape.30), calls=%async_computation | async-start | bytes 786432 | tf_op jit(solution)/shard_map/all_to_all | solution.py:50
  59.0 12.1 %all-to-all-start.1 = ((bf16[2,256,768]{2,1,0:T(8,128)(2,1)}), bf16[2,256,768]{2,1,0:T(8,128)(2,1)S(1)}, u32[]{:S(2)}, u32[]{:S(2)}) async-start(bf16[2,256,768]{2,1,0:T(8,128)(2,1)} %pad_maximum_fusion), calls=%async_computation.1 | async-start | bytes 1572864 | tf_op jit(solution)/shard_map/all_to_all | solution.py:10
  71.2 5.3 %copy-start.3 = (bf16[2,256,768]{2,1,0:T(8,128)(2,1)}, bf16[2,256,768]{2,1,0:T(8,128)(2,1)S(1)}, u32[]{:S(2)}) copy-start(bf16[2,256,768]{2,1,0:T(8,128)(2,1)S(1)} %all-to-all-done.1) | copy-start | bytes 2359300
  76.5 1.4 %copy-start.5 = (bf16[512,1536]{1,0:T(8,128)(2,1)}, bf16[512,1536]{1,0:T(8,128)(2,1)S(1)}, u32[]{:S(2)}) copy-start(bf16[512,1536]{1,0:T(8,128)(2,1)S(1)} %fusion.6) | copy-start | bytes 4718596
  77.9 1.1 %copy-start.1 = (f32[2,256,768]{2,1,0:T(8,128)}, f32[2,256,768]{2,1,0:T(8,128)S(1)}, u32[]{:S(2)}) copy-start(f32[2,256,768]{2,1,0:T(8,128)S(1)} %fusion.9) | copy-start | bytes 4718596
  79.1 12.3 %copy-start.2 = (bf16[512,768]{1,0:T(8,128)(2,1)S(1)}, bf16[512,768]{1,0:T(8,128)(2,1)}, u32[]{:S(2)}) copy-start(bf16[512,768]{1,0:T(8,128)(2,1)} %all_gather.3) | copy-start | bytes 2359300
  80.0 2.6 %collective-permute-start = (f32[256,768]{1,0:T(8,128)}, f32[256,768]{1,0:T(8,128)}, u32[]{:S(2)}, u32[]{:S(2)}) collective-permute-start(f32[256,768]{1,0:T(8,128)} %dynamic-slice_bitcast_fusion), channel_id=1, source_target_pairs={{0,1},{1,0},{2,3},{3,2},{4,5},{5,4},{6,7},{7,6},{8,9},{9,8},{10,11... | collective-permute-start | bytes 2359304 | tf_op jit(solution)/shard_map/ppermute | solution.py:59
  85.0 23.0 %all-to-all-start.3 = ((bf16[128,2,768]{2,1,0:T(2,128)(2,1)}), bf16[128,2,768]{2,1,0:T(2,128)(2,1)S(1)}, u32[]{:S(2)}, u32[]{:S(2)}) async-start(bf16[128,2,768]{2,1,0:T(2,128)(2,1)} %reshape.34), calls=%async_computation.3 | async-start | bytes 786432 | tf_op jit(solution)/shard_map/all_to_all | solution.py:64
  91.4 4.4 %copy-start.4 = (bf16[2,256,768]{2,1,0:T(8,128)(2,1)S(1)}, bf16[2,256,768]{2,1,0:T(8,128)(2,1)}, u32[]{:S(2)}) copy-start(bf16[2,256,768]{2,1,0:T(8,128)(2,1)} %copy-done.3) | copy-start | bytes 2359300
  91.4 4.4 %copy-start.6 = (f32[512,1536]{1,0:T(8,128)S(1)}, f32[512,1536]{1,0:T(8,128)}, u32[]{:S(2)}) copy-start(f32[512,1536]{1,0:T(8,128)} %fusion.11) | copy-start | bytes 9437188
